TPU v7x, 256 devices: a whole 4x4x8 slice. The times are simulated.
256 devices in a mesh: corpus: 32 (over x, y, core), fsdp: 8 (over z).
Axes of the slice: x: 4, y: 4, z: 8, core: 2. Of those that a mesh axis runs over, the one named last changes fastest.
Arguments:
- queries: bfloat16 [1024, 2048], P(('corpus', 'fsdp')), may hold values from -16 to 16
- candidates: int32 [1024, 8], P(('corpus', 'fsdp')), may hold values from 0 to 1023, as said below
- tables: bfloat16 [1024, 20, 2048], P('corpus'), may hold values from -6 to 6
- lengths: int32 [1024], P('corpus'), may hold values from 5 to 20
- passage_embed: bfloat16 [1024, 2048], P('corpus'), may hold values from -6 to 6
- reader_weight: bfloat16 [2048, 2560], P(('corpus', 'fsdp')), may hold values from -0.125 to 0.125
- readout: float32 [2560], replicated, may hold values from -0.125 to 0.125
Outputs:
- query_grad: float32 [1024, 2048], P(('corpus', 'fsdp'))
- losses: float32 [1024], P(('corpus', 'fsdp'))
Inputs may be any that keep to these rules, and one draw needn't show every extreme that they name: Tables 32 * j to 32 * j + 31 are held by index j of corpus. Among the 32 candidates of one device's queries at most 2 are held by any one index of corpus, and one index of corpus holds exactly 2 of every device's candidates.
All inputs are finite; a program needn't handle non-finite values.
Results may differ from a plain program's by a relative error of at most 0.0021.
Values may be sent and summed in bfloat16 or wider, within the bound.
A program may use at most 128 MiB of HBM per device.

v0:
```python
import math

import jax
import jax.numpy as jnp
from jax import lax
from jax.sharding import PartitionSpec as P

GELU_SCALE = math.sqrt(2.0 / math.pi)
GELU_CUBIC = 0.044715
LOSS_SCALE = 64.0


def gelu_pair(hidden):
    tanh_part = jnp.tanh(GELU_SCALE * (hidden + GELU_CUBIC * hidden * hidden * hidden))
    values = 0.5 * hidden * (1.0 + tanh_part)
    slopes = 0.5 * (1.0 + tanh_part) + 0.5 * hidden * (1.0 - tanh_part * tanh_part) * GELU_SCALE * (
        1.0 + 3.0 * GELU_CUBIC * hidden * hidden
    )
    return (values, slopes)


def read_tables(table_rows, table_lens, query_rows, weight, readout):
    count_rows, tok_len, width = table_rows.shape
    inputs = (table_rows.astype(jnp.float32) + query_rows.astype(jnp.float32)[:, None, :]).astype(
        jnp.bfloat16
    )
    hidden = jnp.dot(
        inputs.reshape(count_rows * tok_len, width), weight, preferred_element_type=jnp.float32
    )
    values, slopes = gelu_pair(hidden)
    readings = jnp.dot(values, readout, precision=lax.Precision.HIGHEST).reshape(
        count_rows, tok_len
    )
    positions = lax.broadcasted_iota(jnp.int32, (count_rows, tok_len), 1)
    valid_tok = (positions < table_lens[:, None]).astype(jnp.float32)
    weights_tok = valid_tok / table_lens[:, None].astype(jnp.float32)
    likeness = jnp.sum(weights_tok * readings, axis=1)
    summed = (
        jnp.einsum(
            "mt,mtn->mn",
            weights_tok,
            slopes.reshape(count_rows, tok_len, -1),
            precision=lax.Precision.HIGHEST,
        )
        * readout[None, :]
    )
    towards = jnp.dot(summed.astype(jnp.bfloat16), weight.T, preferred_element_type=jnp.float32)
    return (likeness, towards)


def score_rows(query_rows, embeds):
    products = query_rows.astype(jnp.float32) * embeds.astype(jnp.float32)
    return jnp.sum(products, axis=1) / math.sqrt(embeds.shape[1])


def finish(scores, likeness, embeds, towards, query_count):
    width = embeds.shape[1]
    retrieve = scores.reshape(query_count, -1)
    joined = retrieve + likeness.reshape(query_count, -1)
    prior_prob = jax.nn.softmax(retrieve, axis=1)
    posterior = jax.nn.softmax(joined, axis=1)
    losses = jax.nn.logsumexp(retrieve, axis=1) - jax.nn.logsumexp(joined, axis=1)
    factors = (prior_prob - posterior) / math.sqrt(width)
    emb_three = embeds.astype(jnp.float32).reshape(query_count, -1, width)
    tow_three = towards.reshape(query_count, -1, width)
    first_part = jnp.einsum("qk,qkd->qd", factors, emb_three, precision=lax.Precision.HIGHEST)
    second_part = jnp.einsum("qk,qkd->qd", posterior, tow_three, precision=lax.Precision.HIGHEST)
    return (LOSS_SCALE * (first_part - second_part), losses)


def on_device(queries, candidates, tables, lengths, passage_embed, reader_weight, readout):
    query_count, cand_count = candidates.shape
    per_device = query_count * cand_count
    tab_dev = tables.shape[0]
    owners_count = lax.axis_size("corpus")
    capacity = max(2, 2 * per_device // owners_count)
    slot_count = owners_count * capacity
    weight = lax.all_gather(reader_weight, ("corpus", "fsdp"), axis=0, tiled=True)
    flat_ids = candidates.reshape(per_device)
    owner_idx = flat_ids // tab_dev
    local_ids = flat_ids % tab_dev
    row_pos = lax.broadcasted_iota(jnp.int32, (per_device, per_device), 0)
    col_pos = lax.broadcasted_iota(jnp.int32, (per_device, per_device), 1)
    same_owner = (owner_idx[:, None] == owner_idx[None, :]) & (col_pos < row_pos)
    earlier = jnp.sum(same_owner.astype(jnp.int32), axis=1)
    slot_of = owner_idx * capacity + earlier
    slot_match = slot_of[:, None] == jnp.arange(slot_count, dtype=jnp.int32)[None, :]
    slot_ids = jnp.sum(jnp.where(slot_match, local_ids[:, None], 0), axis=0).reshape(
        owners_count, capacity
    )
    query_rows = jnp.repeat(queries, cand_count, axis=0)
    asked_ids = lax.all_to_all(slot_ids, "corpus", split_axis=0, concat_axis=0, tiled=True)
    got_tables = lax.all_to_all(
        tables[asked_ids], "corpus", split_axis=0, concat_axis=0, tiled=True
    )
    got_embeds = lax.all_to_all(
        passage_embed[asked_ids], "corpus", split_axis=0, concat_axis=0, tiled=True
    )
    got_lengths = lax.all_to_all(
        lengths[asked_ids], "corpus", split_axis=0, concat_axis=0, tiled=True
    )
    width = got_embeds.shape[-1]
    embeds = got_embeds.reshape(slot_count, width)[slot_of]
    picked_tables = got_tables.reshape(slot_count, -1, width)[slot_of]
    picked_lengths = got_lengths.reshape(slot_count)[slot_of]
    likeness, towards = read_tables(picked_tables, picked_lengths, query_rows, weight, readout)
    scores = score_rows(query_rows, embeds)
    return finish(scores, likeness, embeds, towards, query_count)


def solution(mesh):
    in_specs = (
        P(("corpus", "fsdp"), None),
        P(("corpus", "fsdp"), None),
        P("corpus", None, None),
        P("corpus"),
        P("corpus", None),
        P(("corpus", "fsdp"), None),
        P(),
    )
    out_specs = (P(("corpus", "fsdp"), None), P(("corpus", "fsdp")))
    return jax.shard_map(
        on_device, mesh=mesh, in_specs=in_specs, out_specs=out_specs, check_vma=False
    )
```

profile of v0, /device:TPU:8, one launch (start us, length us, event | category | flops | bytes accessed | tf_op | source)
XLA Modules:
  0.0 241.4 jit_solution(13516622778680595161)
XLA Ops:
  7.2 0.0 copy-start
  7.2 0.0 copy-start.2
  7.2 0.0 all-gather.2.cloned.1.call-start
  7.2 0.7 all-gather.2.cloned.1.call-update
  7.9 0.8 reshape.269
  8.8 0.2 convert_reduce_fusion
  8.9 0.1 select_reduce_fusion
  9.0 0.1 all_to_all.20
  9.1 13.5 %all_to_all.31 = s32[32,1,2]{2,1,0:T(1,128)S(1)} all-to-all(s32[32,1,2]{2,1,0:T(1,128)S(1)} %bitcast.54), channel_id=1, replica_groups=mesh['corpus'=32,'fsdp'=8] {'corpus'}, dimensions={0} | all-to-all | bytes 512 | tf_op jit(solution)/shard_map/all_to_all | solution.py:92
  22.6 0.1 copy.21
  22.7 0.1 copy.22
  22.8 0.1 reshape.280
  22.9 0.0 copy-done.2
  22.9 0.0 copy-start.3
  22.9 0.8 gather_fusion.2
  23.7 0.7 all_to_all.24
  24.4 4.9 %all-to-all-start.2 = ((s32[32,1,2]{2,1,0:T(1,128)}), s32[32,1,2]{2,1,0:T(1,128)S(1)}, u32[]{:S(2)}, u32[]{:S(2)}) async-start(s32[32,1,2]{2,1,0:T(1,128)} %bitcast.5), calls=%async_computation.2 | async-start | bytes 32768 | tf_op jit(solution)/shard_map/all_to_all | solution.py:99
  29.4 0.0 copy-done.3
  29.4 0.7 gather_fusion
  30.2 0.9 reshape.279
  31.0 4.5 %all-to-all-done.2 = s32[32,1,2]{2,1,0:T(1,128)S(1)} async-done(((s32[32,1,2]{2,1,0:T(1,128)}), s32[32,1,2]{2,1,0:T(1,128)S(1)}, u32[]{:S(2)}, u32[]{:S(2)}) %all-to-all-start.2) | async-done | bytes 288 | tf_op jit(solution)/shard_map/all_to_all | solution.py:99
  35.6 5.5 %all-to-all-start.1 = ((bf16[32,2,2048]{2,1,0:T(2,128)(2,1)}), bf16[32,2,2048]{2,1,0:T(2,128)(2,1)S(1)}, u32[]{:S(2)}, u32[]{:S(2)}) async-start(bf16[32,2,2048]{2,1,0:T(2,128)(2,1)} %reshape.279), calls=%async_computation.1 | async-start | bytes 524288 | tf_op jit(solution)/shard_map/all_to_all | solution.py:96
  41.1 0.0 copy-done
  41.1 18.1 %gather_fusion.4 = bf16[64,20,2048]{2,0,1:T(8,128)(2,1)} fusion(bf16[32,20,2048]{2,0,1:T(8,128)(2,1)S(1)} %copy-done, s32[1024]{0:T(1024)S(1)} %pad_clamp_fusion.1), kind=kCustom, calls=%fused_computation.4 | custom fusion | bytes 10486016 | tf_op jit(solution)/shard_map/gather | solution.py:94
  59.2 9.2 %reshape.311 = bf16[32,2,20,2048]{3,1,0,2:T(2,128)(2,1)} reshape(bf16[64,20,2048]{2,0,1:T(8,128)(2,1)} %gather_fusion.4) | data formatting | bytes 10485760 | tf_op jit(solution)/shard_map/gather | solution.py:94
  68.4 10.6 %copy.24 = bf16[32,2,20,2048]{3,1,2,0:T(2,128)(2,1)} copy(bf16[32,2,20,2048]{3,1,0,2:T(2,128)(2,1)} %reshape.311) | data formatting | bytes 10485760 | tf_op jit(solution)/shard_map/gather | solution.py:94
  79.0 0.0 copy-start.6
  79.0 0.0 all-to-all-done.1
  79.0 8.1 %all-to-all-start.3 = ((bf16[32,2,20,2048]{3,1,2,0:T(2,128)(2,1)}), bf16[32,2,20,2048]{3,1,2,0:T(2,128)(2,1)}, u32[]{:S(2)}, u32[]{:S(2)}) async-start(bf16[32,2,20,2048]{3,1,2,0:T(2,128)(2,1)} %copy.24), calls=%async_computation.3 | async-start | bytes 10485760 | tf_op jit(solution)/shard_map/all_to_all | solution.py:93
  87.1 0.0 copy-done.6
  87.1 0.1 reshape.271
  87.2 0.0 copy-done.5
  87.2 0.0 copy-done.4
  87.3 0.5 broadcast.295
  87.8 0.7 reduce.9
  88.5 0.1 reshape.272
  88.6 0.7 gather_fusion.3
  89.3 0.1 reshape.270
  89.4 0.7 gather_fusion.1
  90.1 0.1 multiply_reduce_fusion
  90.2 0.1 div.68
  90.3 0.1 reduce_max.16
  90.4 77.2 %all-to-all-done.3 = bf16[32,2,20,2048]{3,1,2,0:T(2,128)(2,1)} async-done(((bf16[32,2,20,2048]{3,1,2,0:T(2,128)(2,1)}), bf16[32,2,20,2048]{3,1,2,0:T(2,128)(2,1)}, u32[]{:S(2)}, u32[]{:S(2)}) %all-to-all-start.3) | async-done | bytes 5242912 | tf_op jit(solution)/shard_map/all_to_all | solution.py:93
  167.6 7.8 %copy.25 = bf16[32,2,20,2048]{3,2,1,0:T(8,128)(2,1)} copy(bf16[32,2,20,2048]{3,1,2,0:T(2,128)(2,1)} %all-to-all-done.3) | data formatting | bytes 10485760 | tf_op jit(solution)/shard_map/all_to_all | solution.py:93
  175.4 5.2 %gather_fusion.5 = bf16[32,20,2048]{2,1,0:T(8,128)(2,1)} fusion(bf16[64,20,2048]{2,1,0:T(8,128)(2,1)} %bitcast.52, s32[1024]{0:T(1024)S(1)} %pad_clamp_fusion), kind=kCustom, calls=%fused_computation.5 | custom fusion | bytes 5243008 | tf_op jit(solution)/shard_map/gather | solution.py:104
  180.6 4.5 %add_convert_fusion = bf16[32,20,2048]{2,1,0:T(8,128)(2,1)} fusion(bf16[32,20,2048]{2,1,0:T(8,128)(2,1)} %gather_fusion.5, f32[32,2048]{1,0:T(8,128)S(1)} %broadcast_bitcast_fusion), kind=kLoop, calls=%fused_computation.15 | loop fusion | flops 3932160 | bytes 5505024 | tf_op jit(solution)/shard_map/convert_element_type | solution.py:24
  185.1 3.6 %convert_element_type.56 = bf16[640,2048]{1,0:T(8,128)(2,1)S(1)} reshape(bf16[32,20,2048]{2,1,0:T(8,128)(2,1)} %add_convert_fusion) | data formatting | bytes 5242880 | tf_op jit(solution)/shard_map/convert_element_type | solution.py:24
  188.7 0.0 all-gather.2.cloned.1.call-done
  188.8 14.2 %fusion.4 = (f32[640,2560]{1,0:T(8,128)}, f32[640,2560]{1,0:T(8,128)S(1)}) fusion(bf16[640,2048]{1,0:T(8,128)(2,1)S(1)} %convert_element_type.56, bf16[2048,2560]{1,0:T(8,128)(2,1)} %all-gather.2.cloned.1.call-done), kind=kOutput, calls=%fused_computation.12 | convolution fusion | flops 6738739200 | bytes 26214400 | tf_op jit(solution)/shard_map/dot_general | solution.py:27
  203.0 7.3 %fusion.14 = f32[640]{0:T(1024)S(1)} fusion(f32[2560,1]{0,1:T(1,128)S(1)} %reshape.330, f32[640,2560]{1,0:T(8,128)S(1)} %get-tuple-element.17), kind=kOutput, calls=%fused_computation.23 | convolution fusion | flops 32768000 | bytes 6566400 | tf_op jit(solution)/shard_map/dot_general | solution.py:31
  210.4 0.1 reshape.274
  210.5 0.2 convert_divide_fusion
  210.7 0.1 reshape.275
  210.8 0.2 fusion.34
  211.0 7.6 %reshape.276 = f32[32,20,2560]{2,1,0:T(8,128)} reshape(f32[640,2560]{1,0:T(8,128)} %get-tuple-element.16) | data formatting | bytes 13107200 | tf_op jit(solution)/shard_map/reshape | solution.py:42
  218.6 0.2 exponential_reduce_fusion
  218.8 0.1 fusion.24
  218.9 0.3 fusion.20
  219.1 0.5 add_subtract_fusion
  219.7 6.4 %fusion.35 = f32[32,1,2560]{2,1,0:T(1,128)S(1)} fusion(f32[32,20,1]{1,2,0:T(1,128)S(1)} %bitcast.53, f32[32,20,2560]{2,1,0:T(8,128)} %reshape.276), kind=kOutput, calls=%fused_computation.75 | convolution fusion | flops 19660800 | bytes 6883840 | tf_op jit(solution)/shard_map/mt,mtn->mn/dot_general | solution.py:39
  226.1 7.1 %convolution_bitcast_fusion = f32[4,8,2048]{2,1,0:T(8,128)S(1)} fusion(bf16[2048,2560]{1,0:T(8,128)(2,1)} %all-gather.2.cloned.1.call-done, f32[32,1,2560]{2,1,0:T(1,128)S(1)} %fusion.35, f32[2560]{0:T(1024)S(1)} %copy-done.4), kind=kOutput, calls=%fused_computation.22 | convolution fusion | flops 335708160 | bytes 11085824 | tf_op jit(solution)/shard_map/dot_general | solution.py:47
  233.2 0.4 fusion.36
  233.6 0.6 fusion.22
  234.2 0.0 copy-done.1
  (16 shorter events, 0.1 us)
Async XLA Ops:
  7.2 33.9 %copy-start = (bf16[32,20,2048]{2,0,1:T(8,128)(2,1)S(1)}, bf16[32,20,2048]{2,0,1:T(8,128)(2,1)}, u32[]{:S(2)}) copy-start(bf16[32,20,2048]{2,0,1:T(8,128)(2,1)} %param.9) | copy-start | bytes 7864324
  7.2 15.7 %copy-start.2 = (s32[32]{0:T(128)S(1)}, s32[32]{0:T(128)}, u32[]{:S(2)}) copy-start(s32[32]{0:T(128)} %param.10) | copy-start | bytes 388
  7.2 181.6 %all-gather.2.cloned.1.call-start = ((), (), s32[]{:S(2)}) async-start(), calls=%async_computation.4 | async-start | bytes 10526720 | tf_op jit(solution)/shard_map/all_gather | solution.py:78
  22.9 6.5 %copy-start.3 = (bf16[32,2048]{1,0:T(8,128)(2,1)S(1)}, bf16[32,2048]{1,0:T(8,128)(2,1)}, u32[]{:S(2)}) copy-start(bf16[32,2048]{1,0:T(8,128)(2,1)} %param.11) | copy-start | bytes 393220
  24.4 11.1 %all-to-all-start.2 = ((s32[32,1,2]{2,1,0:T(1,128)}), s32[32,1,2]{2,1,0:T(1,128)S(1)}, u32[]{:S(2)}, u32[]{:S(2)}) async-start(s32[32,1,2]{2,1,0:T(1,128)} %bitcast.5), calls=%async_computation.2 | async-start | bytes 32768 | tf_op jit(solution)/shard_map/all_to_all | solution.py:99
  35.6 43.4 %all-to-all-start.1 = ((bf16[32,2,2048]{2,1,0:T(2,128)(2,1)}), bf16[32,2,2048]{2,1,0:T(2,128)(2,1)S(1)}, u32[]{:S(2)}, u32[]{:S(2)}) async-start(bf16[32,2,2048]{2,1,0:T(2,128)(2,1)} %reshape.279), calls=%async_computation.1 | async-start | bytes 524288 | tf_op jit(solution)/shard_map/all_to_all | solution.py:96
  79.0 8.1 %copy-start.6 = (s32[4,8]{1,0:T(4,128)S(1)}, s32[4,8]{1,0:T(4,128)}, u32[]{:S(2)}) copy-start(s32[4,8]{1,0:T(4,128)} %param.8) | copy-start | bytes 388
  79.0 8.2 %copy-start.5 = (bf16[4,2048]{1,0:T(4,128)(2,1)S(1)}, bf16[4,2048]{1,0:T(4,128)(2,1)}, u32[]{:S(2)}) copy-start(bf16[4,2048]{1,0:T(4,128)(2,1)} %param.7) | copy-start | bytes 49156
  79.0 8.2 %copy-start.4 = (f32[2560]{0:T(1024)S(1)}, f32[2560]{0:T(1024)}, u32[]{:S(2)}) copy-start(f32[2560]{0:T(1024)} %param.13) | copy-start | bytes 30724
  79.0 88.6 %all-to-all-start.3 = ((bf16[32,2,20,2048]{3,1,2,0:T(2,128)(2,1)}), bf16[32,2,20,2048]{3,1,2,0:T(2,128)(2,1)}, u32[]{:S(2)}, u32[]{:S(2)}) async-start(bf16[32,2,20,2048]{3,1,2,0:T(2,128)(2,1)} %copy.24), calls=%async_computation.3 | async-start | bytes 10485760 | tf_op jit(solution)/shard_map/all_to_all | solution.py:93
  219.7 14.6 %copy-start.1 = (bf16[32,20,2048]{2,0,1:T(8,128)(2,1)S(1)}, bf16[32,20,2048]{2,0,1:T(8,128)(2,1)}, u32[]{:S(2)}) copy-start(bf16[32,20,2048]{2,0,1:T(8,128)(2,1)} %param.9) | copy-start | bytes 7864324
Sparse Core Ops, SparseCore 0:
  11.6 157.4 all-gather.1
where the time goes:
time: 245 us; the launch traced here: 241 us
  waiting for transfers between devices  82.4 us (34%)
  local copies, waits for them, and re-layouts  68.9 us (28%)
  matrix products  35.8 us (15%)
  starting transfers between devices  18.6 us (8%)
  between operations  14.5 us (6%)
  blocking collectives  13.5 us (6%)
  other arithmetic  7.68 us (3%)
    all_to_all x1, waiting for transfers between devices, on_device(): lax.all_to_all(tables[asked_ids], 'corpus', split_axis=0, concat_axis=0,...  77.2 us
    gather x3, local copies, waits for them, and re-layouts, on_device(): tables[asked_ids]  37.9 us
    dot_general x1, matrix products, read_tables(): jnp.dot(inputs.reshape(count_rows * tok_len, width), weight, preferred_el...  14.2 us
    all_to_all x1, blocking collectives, on_device(): lax.all_to_all(slot_ids, 'corpus', split_axis=0, concat_axis=0, tiled=True)  13.5 us
    all_to_all x1, starting transfers between devices, on_device(): lax.all_to_all(tables[asked_ids], 'corpus', split_axis=0, concat_axis=0,...  8.07 us
    all_to_all x1, local copies, waits for them, and re-layouts, on_device(): lax.all_to_all(tables[asked_ids], 'corpus', split_axis=0, concat_axis=0,...  7.77 us
    reshape x1, local copies, waits for them, and re-layouts, read_tables(): slopes.reshape(count_rows, tok_len, -1)  7.57 us
    dot_general x1, matrix products, read_tables(): jnp.dot(values, readout, precision=lax.Precision.HIGHEST)  7.35 us
  transfers between devices with their start and end apart: 4, of which 2 were waited for; matrix products, arithmetic and copies ran while one was open for 27% of the time, Pallas kernels for 0%

commit v1 on v0

v1 whole, which is shorter than its diff:
```python
import functools
import math

import jax
import jax.numpy as jnp
from jax import lax
from jax.experimental import pallas as pl
from jax.experimental.pallas import tpu as pltpu
from jax.sharding import PartitionSpec as P

GELU_SCALE = math.sqrt(2.0 / math.pi)
GELU_CUBIC = 0.044715
LOSS_SCALE = 64.0
BETA = GELU_CUBIC / (GELU_SCALE * GELU_SCALE)
FAR = -1.0e5

MESH = pl.DeviceIdType.MESH
F32 = jnp.float32
BF16 = jnp.bfloat16
I32 = jnp.int32
NJ, NF = 32, 8
HID = 320
LANES = 384
SLOTS = NJ * 2


def iota(shape, dim):
    return lax.broadcasted_iota(I32, shape, dim)


def dot_nt(a, b):
    return lax.dot_general(a, b, (((1,), (1,)), ((), ())), preferred_element_type=F32)


def dot(a, b):
    return jnp.dot(a, b, preferred_element_type=F32)


def two(x):
    hi = x.astype(BF16)
    return hi, (x - hi.astype(F32)).astype(BF16)


def kernel(
    w_ref, q_ref, cand_ref, tab_ref, len_ref, emb_ref, ro_ref,
    grad_ref, loss_ref,
    wsl, ros, qz, wall, w2, x_s, tw0, tw, qw, linv, cidv, cid, emb32, lens_s, e32, esend, eall, acc, lvs, rsend, rall,
    zrow, zall, outp, orec,
    ws_sem, wr_sem, qs_sem, qr_sem, gs_sem, gr_sem, hs_sem, hr_sem, es_sem, er_sem, rs_sem, rr_sem,
    ls_sem, lr_sem, os_sem, or_sem, c_sem,
):
    j = lax.axis_index("corpus")
    f = lax.axis_index("fsdp")
    jx, jy, jc = j // 8, (j // 2) % 4, j % 2

    def remote(src, dst, ssem, rsem, jj, ff):
        return pltpu.make_async_remote_copy(
            src_ref=src, dst_ref=dst, send_sem=ssem, recv_sem=rsem, device_id=(jj, ff), device_id_type=MESH
        )

    load = pltpu.make_async_copy(tab_ref, x_s, c_sem.at[5])
    load.start()
    barrier = pltpu.get_barrier_semaphore()

    @pl.loop(1, NF)
    def _(i):
        pl.semaphore_signal(barrier, inc=1, device_id=(j, (f + i) % NF), device_id_type=MESH)

    @pl.loop(1, NJ)
    def _(i):
        pl.semaphore_signal(barrier, inc=1, device_id=((j + i) % NJ, f), device_id_type=MESH)

    cand = cand_ref[...].astype(F32)
    wide = jnp.concatenate([jnp.broadcast_to(cand[i : i + 1], (8, 8)) for i in range(4)], axis=0)
    eye = iota((32, 32), 0) == iota((32, 32), 1)
    idc = jnp.sum(jnp.where(iota((32, 8), 0) % 8 == iota((32, 8), 1), wide, 0.0), axis=1, keepdims=True)
    idr = jnp.sum(jnp.where(eye, idc, 0.0), axis=0, keepdims=True).astype(I32)
    idc = idc.astype(I32)
    own_r, own_c = idr // 32, idc // 32
    same = (own_c == own_r) & (iota((32, 32), 1) < iota((32, 32), 0))
    earlier = jnp.sum(jnp.where(same, 1, 0).astype(F32), axis=1, keepdims=True).astype(I32)
    lane_of = own_c * 2 + earlier + HID
    at_slot = lane_of == iota((32, LANES), 1)
    id_lane = jnp.sum(jnp.where(at_slot, (idc % 32 + 1).astype(F32), 0.0), axis=0, keepdims=True) - 1.0
    q_lane = jnp.sum(jnp.where(at_slot, (iota((32, LANES), 0) // 8).astype(F32), 0.0), axis=0, keepdims=True)
    row8, lane8 = iota((8, LANES), 0), iota((8, LANES), 1)
    tail = jnp.where(row8 == 0, id_lane, jnp.where(row8 == 1, q_lane, 0.0))
    w_own = w_ref[...].astype(F32)
    for g in range(NF):
        base, off = g * HID // 128 * 128, g * HID % 128
        seg, b = w_own[:, base : base + LANES], base // 128
        rseg = jnp.concatenate([jnp.broadcast_to(ro_ref[b + i : b + i + 1], (8, 128)) for i in range(3)], axis=1)
        if off:
            seg, rseg = pltpu.roll(seg, LANES - off, 1), pltpu.roll(rseg, LANES - off, 1)
        wsl[g] = jnp.where(lane8 < HID, seg, tail).astype(BF16)
        ros[g] = jnp.where(lane8 < HID, rseg, 0.0)
    len_col = jnp.sum(jnp.where(eye, len_ref[...].astype(F32), 0.0), axis=1, keepdims=True)
    lens_s[...] = jnp.broadcast_to(len_col, (32, 128))
    linv[...] = 1.0 / lens_s[...]
    emb32[...] = emb_ref[:, pl.ds(pl.multiple_of(f * 256, 256), 256)].astype(F32)

    pl.semaphore_wait(barrier, NF - 1 + NJ - 1)

    @pl.loop(1, NF)
    def _(i):
        g = (f + i) % NF
        remote(wsl.at[g], wall.at[j, f], ws_sem.at[g], wr_sem.at[f], j, g).start()

    @pl.loop(1, NF)
    def _(i):
        g = (f + i) % NF
        remote(q_ref, qz.at[f], qs_sem.at[g], qr_sem.at[f], j, g).start()

    own_w = pltpu.make_async_copy(wsl.at[f], wall.at[j, f], c_sem.at[0])
    own_q = pltpu.make_async_copy(q_ref, qz.at[f], c_sem.at[1])
    own_w.start()
    own_q.start()

    own_w.wait()

    @pl.loop(1, NF)
    def _(i):
        g = (f + i) % NF
        remote(wsl.at[g], wall.at[j, g], ws_sem.at[g], wr_sem.at[g], j, g).wait_recv()

    def at(x, y, c):
        return ((x + 4) % 4) * 8 + ((y + 4) % 4) * 2 + c

    def along(a, b):
        return at(jx + jnp.where(jc == 0, a, b), jy + jnp.where(jc == 0, b, a), jc)

    def gather(buf, ssem, rsem, width, between):
        sent = []

        def send(slot, part, to):
            if part is None:
                ref, sem = buf.at[slot], rsem.at[slot, 0]
            else:
                ref, sem = buf.at[slot, pl.ds(part * width, width)], rsem.at[slot, part]
            copy = remote(ref, ref, ssem.at[len(sent)], sem, to, f)
            copy.start()
            sent.append(copy)

        def wait(slot, part):
            if part is None:
                ref, sem = buf.at[slot], rsem.at[slot, 0]
            else:
                ref, sem = buf.at[slot, pl.ds(part * width, width)], rsem.at[slot, part]
            remote(ref, ref, ssem.at[0], sem, j ^ 1, f).wait_recv()

        up_a, dn_a, up_b, dn_b, mate = along(1, 0), along(-1, 0), along(0, 1), along(0, -1), at(jx, jy, 1 - jc)

        def first(slot):
            send(slot, None, up_b)
            send(slot, None, dn_b)
            send(slot, None, mate)

        send(j, None, up_a)
        send(j, None, dn_a)
        first(j)
        between()
        wait(dn_a, None)
        send(dn_a, 0, up_a)
        first(dn_a)
        wait(up_a, None)
        send(up_a, 1, dn_a)
        first(up_a)
        over = along(2, 0)

        def second(a):
            wait(along(a, -1), None)
            send(along(a, -1), 0, up_b)
            send(along(a, -1), None, mate)
            wait(along(a, 1), None)
            send(along(a, 1), 1, dn_b)
            send(along(a, 1), None, mate)

        second(0)
        wait(over, 0)
        wait(over, 1)
        first(over)
        second(-1)
        second(1)
        second(2)
        for a in (0, -1, 1, 2):
            wait(along(a, 2), 0)
            wait(along(a, 2), 1)
            send(along(a, 2), None, mate)

        @pl.loop(0, 16)
        def _(k):
            slot = k * 2 + 1 - jc
            remote(buf.at[slot], buf.at[slot], ssem.at[0], rsem.at[slot, 0], j ^ 1, f).wait_recv()

        return sent

    sent_w = gather(wall, gs_sem, gr_sem, 4, lambda: None)

    @pl.loop(0, NJ)
    def _(k):
        for h in range(4):
            pair = jnp.concatenate([wall[k, 2 * h].astype(F32), wall[k, 2 * h + 1].astype(F32)], axis=0)
            w2[pl.ds(pl.multiple_of(k * 64 + h * 16, 16), 16), :] = pair.astype(BF16)

    own_q.wait()

    @pl.loop(1, NF)
    def _(i):
        g = (f + i) % NF
        remote(q_ref, qz.at[g], qs_sem.at[g], qr_sem.at[g], j, g).wait_recv()

    q4 = [qz[g].astype(F32) for g in range(NF)]
    q32 = jnp.concatenate(q4, axis=0).astype(BF16)
    qw[j] = (dot(q32, w2[...]) * GELU_SCALE).reshape(2, 16, LANES)

    pick = (iota((8, 128), 1) == HID - 256 + 2 * j + iota((8, 128), 0)) & (iota((8, 128), 0) < 2)
    cidv[...] = dot_nt(jnp.where(pick, 1.0, 0.0).astype(BF16), w2[:, 256:LANES]).astype(I32)
    to_smem = pltpu.make_async_copy(cidv, cid, c_sem.at[2])
    to_smem.start()
    to_smem.wait()

    def during_queries():
        load.wait()

        @pl.loop(0, 4)
        def _(p):
            rows = pl.ds(pl.multiple_of(p * 160, 16), 160)
            part = dot(x_s[rows, :], w2[...]) * GELU_SCALE
            for b in range(3):
                tw0[b, rows, :] = part[:, b * 128 : (b + 1) * 128]

        @pl.loop(0, 8)
        def _(p):
            for i in range(4):
                c = p * 4 + i
                valid = iota((24, 128), 0).astype(F32) < lens_s[pl.ds(c, 1), :]
                for b in range(3):
                    part = tw0[b, pl.ds(c, 24, stride=32), :]
                    tw[c, :, b * 128 : (b + 1) * 128] = jnp.where(valid, part, FAR)

        @pl.loop(0, NJ)
        def _(i):
            k = (j + i) % NJ
            for s in range(16):
                c = jnp.clip(cid[s % 2, (k * 8 + s // 2) * 8], 0, 31)
                e32[pl.ds(s, 1), :] = emb32[pl.ds(c, 1), :]
            esend[k] = e32[...].astype(BF16)

    sent_q = gather(qw, hs_sem, hr_sem, 1, during_queries)

    @pl.loop(1, NJ)
    def _(i):
        k = (j + i) % NJ
        remote(esend.at[k], eall.at[j], es_sem.at[k], er_sem.at[j], k, f).start()

    own_e = pltpu.make_async_copy(esend.at[j], eall.at[j], c_sem.at[3])
    own_e.start()

    lane16 = iota((16, LANES), 1)
    ro16 = ros[f]
    ro_row = ro16[0:1]

    def send_block(k):
        remote(rsend.at[k], rall.at[j], rs_sem.at[k], rr_sem.at[j], k, f).start()

    @pl.loop(0, NJ)
    def _(i):
        k = (j + i) % NJ
        for s in range(16):
            d, e = s // 2, s % 2
            c = jnp.clip(cid[e, (k * 8 + d) * 8], 0, 31)
            q = jnp.clip(cid[e, (k * 8 + d) * 8 + 1], 0, 3)
            y = tw[c] + qw[k, d // 4, pl.ds((d % 4) * 4 + q, 1), :]
            y2 = y * y
            z = (y * BETA) * y2
            u = y + z
            t = jnp.tanh(u)
            c1 = 1.0 + t
            slope = c1 * ((1.0 - t) * (u + (z + z)) + 1.0)
            value = c1 * y
            slope = slope[0:8] + slope[8:16] + slope[16:24]
            value = (value[0:8] + value[8:16] + value[16:24]) * ro16
            value = value[:, 0:128] + value[:, 128:256] + value[:, 256:384]
            inv = linv[pl.ds(c, 1), :]
            lvs[pl.ds(s, 1), :] = jnp.sum(value, axis=0, keepdims=True) * inv
            slope = jnp.sum(slope, axis=0, keepdims=True)
            for b in range(3):
                acc[pl.ds(s, 1), b * 128 : (b + 1) * 128] = slope[:, b * 128 : (b + 1) * 128] * inv
        like = jnp.sum(lvs[...], axis=1, keepdims=True) * (0.5 / GELU_SCALE)
        summed = (acc[...] * 0.5) * ro_row
        hi = like.astype(BF16).astype(F32)
        mid = (like - hi).astype(BF16).astype(F32)
        low = like - hi - mid
        summed = jnp.where(lane16 == HID, hi, summed)
        summed = jnp.where(lane16 == HID + 1, mid, summed)
        summed = jnp.where(lane16 == HID + 2, low, summed)
        rsend[k] = summed.astype(BF16)

        @pl.when(i > 1)
        def _():
            send_block((j + i - 1) % NJ)

    send_block((j + NJ - 1) % NJ)
    own_r_copy = pltpu.make_async_copy(rsend.at[j], rall.at[j], c_sem.at[4])
    own_r_copy.start()

    own_e.wait()

    @pl.loop(1, NJ)
    def _(i):
        k = (j + i) % NJ
        remote(esend.at[k], eall.at[k], es_sem.at[k], er_sem.at[k], k, f).wait_recv()

    ev = eall[...].reshape(NJ * 16, 256)
    q64 = jnp.concatenate([qz[g, :, pl.ds(pl.multiple_of(f * 256, 256), 256)].astype(F32) for g in range(NF) for _ in range(2)], axis=0)
    sc = dot_nt(q64.astype(BF16), ev)

    r64, s64 = iota((64, 512), 0), iota((64, 512), 1)
    spread = jnp.where(iota((128, 512), 0) == HID - 256 + iota((128, 512), 1) // 16 * 2 + iota((128, 512), 1) % 2, 1.0, 0.0).astype(BF16)
    ids = [wall[j, g, :, 256:LANES].astype(F32) for g in range(NF)]
    id64 = jnp.concatenate([jnp.broadcast_to(v[0:1], (8, 128)) for v in ids], axis=0)
    qi64 = jnp.concatenate([jnp.broadcast_to(v[1:2], (8, 128)) for v in ids], axis=0)
    mine = (dot(id64.astype(BF16), spread) >= 0.0) & (dot(qi64.astype(BF16), spread).astype(I32) == r64 % 4)
    mine = mine & ((s64 // 2) % 8 == r64 // 8)
    score_row = jnp.sum(jnp.where(mine & ((r64 // 4) % 2 == 0), sc, 0.0), axis=0, keepdims=True)

    own_r_copy.wait()

    @pl.loop(1, NJ)
    def _(i):
        k = (j + i) % NJ
        remote(rsend.at[k], rall.at[k], rs_sem.at[k], rr_sem.at[k], k, f).wait_recv()

    rv = rall[...].reshape(NJ * 16, LANES)
    lp = (iota((8, LANES), 1) >= HID) & (iota((8, LANES), 1) < HID + 3)
    like_row = dot_nt(jnp.where(lp, 1.0, 0.0).astype(BF16), rv)[0:1]
    zrow[:, 0:512] = like_row
    zrow[:, 512:1024] = score_row

    @pl.loop(1, NF)
    def _(i):
        g = (f + i) % NF
        remote(zrow, zall.at[f], ls_sem.at[g], lr_sem.at[f], j, g).start()

    zall[f] = zrow[...]

    @pl.loop(1, NF)
    def _(i):
        g = (f + i) % NF
        remote(zrow, zall.at[g], ls_sem.at[g], lr_sem.at[g], j, g).wait_recv()

    total = zall[0]
    for g in range(1, NF):
        total = total + zall[g]
    retrieve = jnp.broadcast_to(total[:, 512:1024], (64, 512)) * (1.0 / math.sqrt(2048.0))
    joined = retrieve + jnp.broadcast_to(total[:, 0:512], (64, 512))

    def softmax(v):
        top = jnp.max(jnp.where(mine, v, -3.0e38), axis=1, keepdims=True)
        ex = jnp.where(mine, jnp.exp(jnp.where(mine, v - top, 0.0)), 0.0)
        norm = jnp.sum(ex, axis=1, keepdims=True)
        return ex / norm, top + jnp.log(norm)

    prior, lse_r = softmax(retrieve)
    post, lse_j = softmax(joined)
    loss = lse_r - lse_j
    own_row = (iota((64, 128), 0) == f * 8 + iota((64, 128), 1)) & (iota((64, 128), 1) < 4)
    loss_ref[...] = jnp.sum(jnp.where(own_row, loss, 0.0), axis=0, keepdims=True)[:, 0:4]

    hi, lo = two(post)
    mix = dot(hi, rv) + dot(lo, rv)
    mix = jnp.where(iota((64, LANES), 1) < HID, mix, 0.0)
    hi, lo = two(mix)
    fhi, flo = two((prior - post) * (LOSS_SCALE / math.sqrt(2048.0)))
    first = dot(fhi, ev) + dot(flo, ev)
    upper = (iota((64, 256), 0) // 4) % 2 == 1
    for b in range(4):
        w_lo, w_hi = w2[b * 256 : (b + 1) * 256, :], w2[1024 + b * 256 : 1024 + (b + 1) * 256, :]
        part = jnp.where(upper, dot_nt(hi, w_hi) + dot_nt(lo, w_hi), dot_nt(hi, w_lo) + dot_nt(lo, w_lo))
        place = ((f % 4) == b) & (upper == (f // 4 == 1))
        part = jnp.where(place, first, 0.0) - LOSS_SCALE * part
        outp[:, :, b * 256 : (b + 1) * 256] = part.reshape(NF, 8, 256)

    @pl.loop(1, NF)
    def _(i):
        g = (f + i) % NF
        remote(outp.at[g], orec.at[f], os_sem.at[g], or_sem.at[f], j, g).start()

    for copy in sent_w + sent_q:
        copy.wait_send()

    @pl.loop(1, NJ)
    def _(i):
        k = (j + i) % NJ
        remote(esend.at[k], eall.at[k], es_sem.at[k], er_sem.at[k], k, f).wait_send()
        remote(rsend.at[k], rall.at[k], rs_sem.at[k], rr_sem.at[k], k, f).wait_send()

    total8 = outp[f]

    @pl.loop(1, NF)
    def _(i):
        g = (f + i) % NF
        remote(wsl.at[g], wall.at[j, g], ws_sem.at[g], wr_sem.at[g], j, g).wait_send()
        remote(q_ref, qz.at[g], qs_sem.at[g], qr_sem.at[g], j, g).wait_send()
        remote(zrow, zall.at[g], ls_sem.at[g], lr_sem.at[g], j, g).wait_send()
        remote(outp.at[g], orec.at[g], os_sem.at[g], or_sem.at[g], j, g).wait()

    orec[f] = total8
    total8 = orec[0]
    for g in range(1, NF):
        total8 = total8 + orec[g]
    grad_ref[:, 0:1024] = total8[0:4]
    grad_ref[:, 1024:2048] = total8[4:8]


def on_device(queries, candidates, tables, lengths, passage_embed, reader_weight, readout):
    vm = pl.BlockSpec(memory_space=pltpu.VMEM)
    dma = pltpu.SemaphoreType.DMA
    grad, loss = pl.pallas_call(
        kernel,
        out_shape=(jax.ShapeDtypeStruct((4, 2048), F32), jax.ShapeDtypeStruct((1, 4), F32)),
        in_specs=[vm] * 3 + [pl.BlockSpec(memory_space=pl.ANY)] + [vm] * 3,
        out_specs=(vm, vm),
        scratch_shapes=[
            pltpu.VMEM((NF, 8, LANES), BF16),
            pltpu.VMEM((NF, 8, LANES), F32),
            pltpu.VMEM((NF, 4, 2048), BF16),
            pltpu.VMEM((NJ, NF, 8, LANES), BF16),
            pltpu.VMEM((2048, LANES), BF16),
            pltpu.VMEM((640, 2048), BF16),
            pltpu.VMEM((3, 768, 128), F32),
            pltpu.VMEM((32, 24, LANES), F32),
            pltpu.VMEM((NJ, 2, 16, LANES), F32),
            pltpu.VMEM((32, 128), F32),
            pltpu.VMEM((8, 2048), I32),
            pltpu.SMEM((8, 2048), I32),
            pltpu.VMEM((32, 256), F32),
            pltpu.VMEM((32, 128), F32),
            pltpu.VMEM((16, 256), F32),
            pltpu.VMEM((NJ, 16, 256), BF16),
            pltpu.VMEM((NJ, 16, 256), BF16),
            pltpu.VMEM((16, LANES), F32),
            pltpu.VMEM((16, 128), F32),
            pltpu.VMEM((NJ, 16, LANES), BF16),
            pltpu.VMEM((NJ, 16, LANES), BF16),
            pltpu.VMEM((1, 1024), F32),
            pltpu.VMEM((NF, 1, 1024), F32),
            pltpu.VMEM((NF, 8, 1024), F32),
            pltpu.VMEM((NF, 8, 1024), F32),
            dma((NF,)), dma((NF,)), dma((NF,)), dma((NF,)),
            dma((48,)), dma((NJ, 2)), dma((48,)), dma((NJ, 2)),
            dma((NJ,)), dma((NJ,)), dma((NJ,)), dma((NJ,)),
            dma((NF,)), dma((NF,)), dma((NF,)), dma((NF,)), dma((6,)),
        ],
        compiler_params=pltpu.CompilerParams(collective_id=0, has_side_effects=True, vmem_limit_bytes=50 << 20),
    )(
        reader_weight,
        queries,
        candidates,
        tables.transpose(1, 0, 2).reshape(640, 2048),
        lengths.reshape(1, 32),
        passage_embed,
        readout.reshape(20, 128),
    )
    return grad, loss.reshape(4)


def solution(mesh):
    both = ("corpus", "fsdp")
    in_specs = (P(both, None), P(both, None), P("corpus", None, None), P("corpus"), P("corpus", None), P(both, None), P())
    return jax.shard_map(
        on_device, mesh=mesh, in_specs=in_specs, out_specs=(P(both, None), P(both)), check_vma=False
    )
```

time: 245 us -> 91.5 us (0.37)
  the two profiles are of different devices: /device:TPU:8 before, /device:TPU:2 now
where the time goes in v1:
time: 91.5 us; the launch traced here: 90.3 us
  Pallas kernels  82.3 us (90%)
  local copies, waits for them, and re-layouts  7.3 us (8%)
    pallas_call x1, Pallas kernels, on_device(): pl.pallas_call(kernel, out_shape=(jax.ShapeDtypeStruct((4, 2048), F32), j...  82.3 us
    unnamed x16, local copies, waits for them, and re-layouts  7.3 us

profile of v1, /device:TPU:2, one launch (start us, length us, event | category | flops | bytes accessed | tf_op | source)
XLA Modules:
  0.0 90.3 jit_solution(13969091706280837425)
XLA Ops:
  0.6 0.0 copy-start
  0.6 1.7 %copy-done = bf16[32,20,2048]{2,0,1:T(8,128)(2,1)S(1)} copy-done((bf16[32,20,2048]{2,0,1:T(8,128)(2,1)S(1)}, bf16[32,20,2048]{2,0,1:T(8,128)(2,1)}, u32[]{:S(2)}) %copy-start) | copy-done | bytes 2621464
  2.4 0.0 copy-start.1
  2.4 0.9 copy-done.1
  3.3 0.0 copy-start.2
  3.3 0.8 copy-done.2
  4.1 0.0 copy-start.3
  4.1 0.7 copy-done.3
  4.8 0.0 copy-start.4
  4.8 0.7 copy-done.4
  5.5 0.0 copy-start.5
  5.5 0.7 copy-done.5
  6.2 0.0 copy-start.6
  6.2 0.7 copy-done.6
  6.8 82.3 %shard_map.86 = (f32[4,2048]{1,0:T(4,128)S(1)}, f32[1,4]{1,0:T(1,128)S(1)}) custom-call(bf16[8,2560]{1,0:T(8,128)(2,1)S(1)} %copy-done.2, bf16[4,2048]{1,0:T(4,128)(2,1)S(1)} %copy-done.3, s32[4,8]{1,0:T(4,128)S(1)} %copy-done.5, bf16[640,2048]{1,0:T(8,128)(2,1)S(1)} %bitcast.6, s32[1,32]{1,0:T(1,128)S(1)} %bitcast.8, bf16[32,2048]{1,0:T(8,128)(2,1)S(1)} %copy-done.1, ...), custom_call_target="tpu_custom_call" | custom-call | tf_op jit(solution)/shard_map/pallas_call | solution.py:419
  89.1 0.6 copy.11
  89.7 0.5 copy.12
Async XLA Ops:
  0.6 1.7 %copy-start = (bf16[32,20,2048]{2,0,1:T(8,128)(2,1)S(1)}, bf16[32,20,2048]{2,0,1:T(8,128)(2,1)}, u32[]{:S(2)}) copy-start(bf16[32,20,2048]{2,0,1:T(8,128)(2,1)} %param.9) | copy-start | bytes 7864324
  2.4 0.9 %copy-start.1 = (bf16[32,2048]{1,0:T(8,128)(2,1)S(1)}, bf16[32,2048]{1,0:T(8,128)(2,1)}, u32[]{:S(2)}) copy-start(bf16[32,2048]{1,0:T(8,128)(2,1)} %emb_ref.1) | copy-start | bytes 393220
  3.3 0.8 copy-start.2
  4.1 0.7 copy-start.3
  4.8 0.7 copy-start.4
  5.5 0.7 copy-start.5
  6.2 0.7 copy-start.6

commit v2 on v1

v2 whole, which is shorter than its diff:
```python
import functools
import math

import jax
import jax.numpy as jnp
from jax import lax
from jax.experimental import pallas as pl
from jax.experimental.pallas import tpu as pltpu
from jax.sharding import PartitionSpec as P

GELU_SCALE = math.sqrt(2.0 / math.pi)
GELU_CUBIC = 0.044715
LOSS_SCALE = 64.0
BETA = GELU_CUBIC / (GELU_SCALE * GELU_SCALE)
FAR = -1.0e5

MESH = pl.DeviceIdType.MESH
F32 = jnp.float32
BF16 = jnp.bfloat16
I32 = jnp.int32
NJ, NF = 32, 8
HID = 320
LANES = 384
SLOTS = NJ * 2


def iota(shape, dim):
    return lax.broadcasted_iota(I32, shape, dim)


def dot_nt(a, b):
    return lax.dot_general(a, b, (((1,), (1,)), ((), ())), preferred_element_type=F32)


def dot(a, b):
    return jnp.dot(a, b, preferred_element_type=F32)


def two(x):
    hi = x.astype(BF16)
    return hi, (x - hi.astype(F32)).astype(BF16)


def kernel(
    w_hbm, q_hbm, cand_hbm, tab_hbm, len_hbm, emb_hbm, ro_hbm,
    grad_ref, loss_ref,
    w_ref, q_ref, cand_ref, len_ref, ro_ref, wsl, ros, qz, wall, w2, x_s, tw0, tw, tw3, qw, linv, cidv, cid, lens_s, emball, ev_s, mine_s, acc, lvs, rsend, rall,
    zrow, zall, srow, sall, outp, orec, tab, qcur,
    ws_sem, wr_sem, qs_sem, qr_sem, gs_sem, gr_sem, hs_sem, hr_sem, es_sem, er_sem, rs_sem, rr_sem,
    ls_sem, lr_sem, os_sem, or_sem, c_sem, i_sem, ss_sem, sr_sem,
):
    j = lax.axis_index("corpus")
    f = lax.axis_index("fsdp")
    jx, jy, jc = j // 8, (j // 2) % 4, j % 2

    def remote(src, dst, ssem, rsem, jj, ff):
        return pltpu.make_async_remote_copy(
            src_ref=src, dst_ref=dst, send_sem=ssem, recv_sem=rsem, device_id=(jj, ff), device_id_type=MESH
        )

    pairs = ((cand_hbm, cand_ref), (w_hbm, w_ref), (ro_hbm, ro_ref), (len_hbm, len_ref), (q_hbm, q_ref))
    pairs = pairs + ((emb_hbm.at[:, pl.ds(pl.multiple_of(f * 256, 256), 256)], emball.at[j]), (tab_hbm, x_s))
    loads = [pltpu.make_async_copy(a, b, i_sem.at[n]) for n, (a, b) in enumerate(pairs)]
    for load in loads:
        load.start()
    barrier = pltpu.get_barrier_semaphore()

    @pl.loop(1, NF)
    def _(i):
        pl.semaphore_signal(barrier, inc=1, device_id=(j, (f + i) % NF), device_id_type=MESH)

    @pl.loop(1, NJ)
    def _(i):
        pl.semaphore_signal(barrier, inc=1, device_id=((j + i) % NJ, f), device_id_type=MESH)

    for load in loads[:6]:
        load.wait()

    cand = cand_ref[...].astype(F32)
    wide = jnp.concatenate([jnp.broadcast_to(cand[i : i + 1], (8, 8)) for i in range(4)], axis=0)
    eye = iota((32, 32), 0) == iota((32, 32), 1)
    idc = jnp.sum(jnp.where(iota((32, 8), 0) % 8 == iota((32, 8), 1), wide, 0.0), axis=1, keepdims=True)
    idr = jnp.sum(jnp.where(eye, idc, 0.0), axis=0, keepdims=True).astype(I32)
    idc = idc.astype(I32)
    own_r, own_c = idr // 32, idc // 32
    same = (own_c == own_r) & (iota((32, 32), 1) < iota((32, 32), 0))
    earlier = jnp.sum(jnp.where(same, 1, 0).astype(F32), axis=1, keepdims=True).astype(I32)
    lane_of = own_c * 2 + earlier + HID
    at_slot = lane_of == iota((32, LANES), 1)
    id_lane = jnp.sum(jnp.where(at_slot, (idc % 32 + 1).astype(F32), 0.0), axis=0, keepdims=True) - 1.0
    q_lane = jnp.sum(jnp.where(at_slot, (iota((32, LANES), 0) // 8).astype(F32), 0.0), axis=0, keepdims=True)
    row8, lane8 = iota((8, LANES), 0), iota((8, LANES), 1)
    tail = jnp.where(row8 == 0, id_lane, jnp.where(row8 == 1, q_lane, 0.0))
    w_own = w_ref[...].astype(F32)
    for g in range(NF):
        base, off = g * HID // 128 * 128, g * HID % 128
        seg, b = w_own[:, base : base + LANES], base // 128
        rseg = jnp.concatenate([jnp.broadcast_to(ro_ref[b + i : b + i + 1], (8, 128)) for i in range(3)], axis=1)
        if off:
            seg, rseg = pltpu.roll(seg, LANES - off, 1), pltpu.roll(rseg, LANES - off, 1)
        wsl[g] = jnp.where(lane8 < HID, seg, tail).astype(BF16)
        ros[g] = jnp.where(lane8 < HID, rseg, pltpu.roll(rseg, 64, 1))
    len_col = jnp.sum(jnp.where(eye, len_ref[...].astype(F32), 0.0), axis=1, keepdims=True)
    lens_s[...] = jnp.broadcast_to(len_col, (32, 128))
    linv[...] = 1.0 / lens_s[...]

    pl.semaphore_wait(barrier, NF - 1 + NJ - 1)

    def at(x, y, c):
        return ((x + 4) % 4) * 8 + ((y + 4) % 4) * 2 + c

    def along(a, b):
        return at(jx + jnp.where(jc == 0, a, b), jy + jnp.where(jc == 0, b, a), jc)

    near = (0, 1, -1, 2)
    chip = {(a, b): along(a, b) for b in near for a in near}
    mate = at(jx, jy, 1 - jc)

    def block_copy(buf, ssem, rsem, slot, n, to):
        return remote(buf.at[slot], buf.at[slot], ssem.at[n], rsem.at[slot], to, f)

    @pl.loop(1, NF)
    def _(i):
        g = (f + i) % NF
        remote(wsl.at[g], wall.at[j, f], ws_sem.at[g], wr_sem.at[f], j, g).start()

    for n, c in enumerate(chip.values()):
        if n:
            block_copy(emball, es_sem, er_sem, j, n, c).start()
    block_copy(emball, es_sem, er_sem, j, 0, mate).start()
    own_w = pltpu.make_async_copy(wsl.at[f], wall.at[j, f], c_sem.at[0])
    own_q = pltpu.make_async_copy(q_ref, qz.at[f], c_sem.at[1])
    own_w.start()
    own_q.start()

    own_w.wait()

    @pl.loop(1, NF)
    def _(i):
        g = (f + i) % NF
        remote(wsl.at[g], wall.at[j, g], ws_sem.at[g], wr_sem.at[g], j, g).wait_recv()

    @pl.loop(1, NF)
    def _(i):
        g = (f + i) % NF
        remote(q_ref, qz.at[f], qs_sem.at[g], qr_sem.at[f], j, g).start()

    sent_w = []

    def send_w(slot, to):
        block_copy(wall, gs_sem, gr_sem, slot, len(sent_w), to).start()
        sent_w.append((slot, to))

    def wait_w(slot):
        block_copy(wall, gs_sem, gr_sem, slot, 0, mate).wait_recv()

    for a in near[1:]:
        send_w(j, chip[a, 0])
    for b in near[1:]:
        send_w(j, chip[0, b])
    send_w(j, mate)
    for n, c in enumerate(chip.values()):
        if n:
            block_copy(emball, es_sem, er_sem, c, 0, mate).wait_recv()
            block_copy(emball, es_sem, er_sem, c, 16 + n, mate).start()
    for a in near[1:]:
        wait_w(chip[a, 0])
        for b in near[1:]:
            send_w(chip[a, 0], chip[0, b])
        send_w(chip[a, 0], mate)
    r64, s64 = iota((64, 512), 0), iota((64, 512), 1)
    spread = jnp.where(iota((128, 512), 0) == HID - 256 + iota((128, 512), 1) // 16 * 2 + iota((128, 512), 1) % 2, 1.0, 0.0).astype(BF16)
    ids = [wall[j, g, :, 256:LANES].astype(F32) for g in range(NF)]
    id64 = jnp.concatenate([jnp.broadcast_to(v[0:1], (8, 128)) for v in ids], axis=0)
    qi64 = jnp.concatenate([jnp.broadcast_to(v[1:2], (8, 128)) for v in ids], axis=0)
    id_of = dot(id64.astype(BF16), spread)
    asker = (s64 // 2) % 8 == r64 // 8
    mine = (id_of >= 0.0) & (dot(qi64.astype(BF16), spread).astype(I32) == r64 % 4) & asker
    mine_s[...] = jnp.where(mine, 1.0, 0.0)
    id_row = jnp.sum(jnp.where(asker & (r64 % 8 == 0), id_of, 0.0), axis=0, keepdims=True)

    @pl.loop(0, 16)
    def _(n):
        block_copy(emball, es_sem, er_sem, n * 2 + 1 - jc, 0, mate).wait_recv()

    for g in range(4):
        hot = (iota((256, 128), 0) // 32 == iota((256, 128), 1) // 16)
        hot = hot & ((iota((256, 128), 0) % 32).astype(F32) == id_row[:, g * 128 : (g + 1) * 128])
        rows = emball[g * 8 : (g + 1) * 8].reshape(256, 256)
        hot = jnp.where(hot, 1.0, 0.0).astype(BF16)
        part = lax.dot_general(hot, rows, (((0,), (0,)), ((), ())), preferred_element_type=F32)
        ev_s[g * 128 : (g + 1) * 128, :] = part.astype(BF16)
    for a in near:
        for b in near[1:]:
            wait_w(chip[a, b])
            send_w(chip[a, b], mate)

    @pl.loop(0, 16)
    def _(n):
        wait_w(n * 2 + 1 - jc)

    @pl.loop(0, NJ)
    def _(k):
        for h in range(4):
            pair = jnp.concatenate([wall[k, 2 * h].astype(F32), wall[k, 2 * h + 1].astype(F32)], axis=0)
            w2[pl.ds(pl.multiple_of(k * 64 + h * 16, 16), 16), :] = pair.astype(BF16)
            for e in range(2):
                tab[pl.ds(k * 8 + 2 * h + e, 1), :] = pair[8 * e : 8 * e + 1, 256:LANES]
                tab[pl.ds(256 + k * 8 + 2 * h + e, 1), :] = pair[8 * e + 1 : 8 * e + 2, 256:LANES]

    own_q.wait()

    @pl.loop(1, NF)
    def _(i):
        g = (f + i) % NF
        remote(q_ref, qz.at[g], qs_sem.at[g], qr_sem.at[g], j, g).wait_recv()

    q4 = [qz[g].astype(F32) for g in range(NF)]
    q32 = jnp.concatenate(q4, axis=0).astype(BF16)
    q_own = dot(q32, w2[...]) * GELU_SCALE
    qw[j, 0:32, :] = q_own[:, 0:128]
    qw[j, 32:64, :] = q_own[:, 128:256]
    third = jnp.where(iota((16, 128), 1) < 64, q_own[0:16, 256:384], pltpu.roll(q_own[16:32, 256:384], 64, 1))
    qw[j, 64:80, :] = third

    pick = (iota((8, 128), 1) == HID - 256 + 2 * j + iota((8, 128), 0)) & (iota((8, 128), 0) < 2)
    asked = dot_nt(jnp.where(pick, 1.0, 0.0).astype(BF16), tab[...].astype(BF16))
    cidv[...] = asked.astype(I32)
    to_smem = pltpu.make_async_copy(cidv, cid, c_sem.at[2])
    to_smem.start()
    sent_q = []

    def send_q(slot, to):
        block_copy(qw, hs_sem, hr_sem, slot, len(sent_q), to).start()
        sent_q.append((slot, to))

    for a in near[1:]:
        send_q(j, chip[a, 0])
    for b in near[1:]:
        send_q(j, chip[0, b])
    send_q(j, mate)

    loads[6].wait()

    @pl.loop(0, 4)
    def _(p):
        rows = pl.ds(pl.multiple_of(p * 160, 16), 160)
        part = dot(x_s[rows, :], w2[...]) * GELU_SCALE
        for b in range(3):
            tw0[b, rows, :] = part[:, b * 128 : (b + 1) * 128]

    @pl.loop(0, 8)
    def _(p):
        for i in range(4):
            c = p * 4 + i
            length = lens_s[pl.ds(c, 1), :]
            valid = iota((24, 128), 0).astype(F32) < length
            for b in range(2):
                tw[c, :, b * 128 : (b + 1) * 128] = jnp.where(valid, tw0[b, pl.ds(c, 24, stride=32), :], FAR)
            row, low = iota((16, 128), 0), iota((16, 128), 1) < 64
            token = jnp.where(low, row, row + 10)
            valid = (row < 10) & (token.astype(F32) < length)
            early, late = tw0[2, pl.ds(c, 16, stride=32), :], tw0[2, pl.ds(c + 320, 16, stride=32), :]
            tw3[c] = jnp.where(valid, jnp.where(low, early, pltpu.roll(late, 64, 1)), FAR)

    for a in near[1:]:
        block_copy(qw, hs_sem, hr_sem, chip[a, 0], 0, mate).wait_recv()
        for b in near[1:]:
            send_q(chip[a, 0], chip[0, b])
        send_q(chip[a, 0], mate)
    to_smem.wait()

    q64 = jnp.concatenate([qz[g, :, pl.ds(pl.multiple_of(f * 256, 256), 256)].astype(F32) for g in range(NF) for _ in range(2)], axis=0)
    sc = dot_nt(q64.astype(BF16), ev_s[...])
    srow[...] = jnp.sum(jnp.where((mine_s[...] > 0.5) & ((r64 // 4) % 2 == 0), sc, 0.0), axis=0, keepdims=True)

    @pl.loop(1, NF)
    def _(i):
        g = (f + i) % NF
        remote(srow, sall.at[f], ss_sem.at[g], sr_sem.at[f], j, g).start()

    lane16 = iota((16, LANES), 1)
    ro16 = ros[f]
    ro_row = ro16[0:1]

    def send_block(k):
        remote(rsend.at[k], rall.at[j], rs_sem.at[k], rr_sem.at[j], k, f).start()

    def pair(y):
        y2 = y * y
        z = (y * BETA) * y2
        u = y + z
        t = jnp.tanh(u)
        c1 = 1.0 + t
        return c1 * ((1.0 - t) * (u + (z + z)) + 1.0), c1 * y

    acc[...] = jnp.zeros_like(acc)
    lvs[...] = jnp.zeros_like(lvs)

    def finish(half, k):
        inv = lvs[half]
        sums = []
        for b in range(4):
            part = [acc[half, b, pl.ds(r, 16, stride=8), :] for r in range(8)]
            part = [part[r] + part[r + 4] for r in range(4)]
            sums.append(((part[0] + part[2]) + (part[1] + part[3])) * inv)
        sums[2] = sums[2] + pltpu.roll(sums[2], 64, 1)
        like = jnp.sum(sums[3], axis=1, keepdims=True) * (0.5 / GELU_SCALE)
        summed = (jnp.concatenate(sums[0:3], axis=1) * 0.5) * ro_row
        hi = like.astype(BF16).astype(F32)
        mid = (like - hi).astype(BF16).astype(F32)
        low = like - hi - mid
        summed = jnp.where(lane16 >= HID, 0.0, summed)
        summed = jnp.where(lane16 == HID, hi, summed)
        summed = jnp.where(lane16 == HID + 1, mid, summed)
        summed = jnp.where(lane16 == HID + 2, low, summed)
        rsend[k] = summed.astype(BF16)

    def is_mate(i):
        return ((i % 2 == 0) & (i > 0)) | (i == NJ - 1)

    def block_at(i):
        p = jnp.where(is_mate(i), jnp.where(i == NJ - 1, 15, i // 2 - 1), (i + 1) // 2)
        t = p - 7
        m = jnp.where(p < 4, p, jnp.where(p < 7, 0, 1 + t % 3))
        n = jnp.where(p < 4, 0, jnp.where(p < 7, p - 3, 1 + t // 3))
        a, b = m + (m // 2) * (1 - 2 * (m % 2)), n + (n // 2) * (1 - 2 * (n % 2))
        c = jnp.where(is_mate(i), 1 - jc, jc)
        return at(jx + jnp.where(c == 0, a, b), jy + jnp.where(c == 0, b, a), c)

    def do_block(i, half):
        k = block_at(i)

        @pl.when(is_mate(i) | ((i + 1) // 2 > 3))
        def _():
            block_copy(qw, hs_sem, hr_sem, k, 0, mate).wait_recv()

        @pl.when((i > 0) & jnp.logical_not(is_mate(i)) & ((i + 1) // 2 > 3))
        def _():
            block_copy(qw, hs_sem, hr_sem, k, 24 + (i + 1) // 2, mate).start()

        qcur[:, 0:128] = qw[k, 0:32, :]
        qcur[:, 128:256] = qw[k, 32:64, :]
        third = qw[k, 64:80, :]
        swap = pltpu.roll(third, 64, 1)
        qcur[0:16, 256:384] = jnp.where(iota((16, 128), 1) < 64, third, swap)
        qcur[16:32, 256:384] = jnp.where(iota((16, 128), 1) < 64, swap, third)
        finish(1 - half, block_at((i + NJ - 1) % NJ))
        for s in range(16):
            d, e = s // 2, s % 2
            c = jnp.clip(cid[e, k * 8 + d], 0, 31)
            q = jnp.clip(cid[e, 256 + k * 8 + d], 0, 3)
            q_row = qcur[pl.ds(d * 4 + q, 1), :]
            slope, value = pair(tw[c] + q_row[:, 0:256])
            slope3, value3 = pair(tw3[c] + q_row[:, 256:384])
            slope = slope[0:8] + slope[8:16] + slope[16:24]
            value = (value[0:8] + value[8:16] + value[16:24]) * ro16[:, 0:256]
            value3 = (value3[0:8] + value3[8:16]) * ro16[:, 256:384]
            at8 = pl.ds(s * 8, 8)
            acc[half, 0, at8, :] = slope[:, 0:128]
            acc[half, 1, at8, :] = slope[:, 128:256]
            acc[half, 2, at8, :] = slope3[0:8] + slope3[8:16]
            acc[half, 3, at8, :] = value[:, 0:128] + value[:, 128:256] + value3
            lvs[half, pl.ds(s, 1), :] = linv[pl.ds(c, 1), :]

        @pl.when(i > 1)
        def _():
            send_block(block_at(i - 1))

    @pl.loop(0, NJ // 2)
    def _(n):
        do_block(2 * n, 0)
        do_block(2 * n + 1, 1)

    finish((NJ - 1) % 2, block_at(NJ - 1))
    own_r_copy = pltpu.make_async_copy(rsend.at[j], rall.at[j], c_sem.at[4])
    own_r_copy.start()
    send_block(block_at(NJ - 1))

    own_r_copy.wait()

    @pl.loop(1, NJ)
    def _(i):
        k = (j + i) % NJ
        remote(rsend.at[k], rall.at[k], rs_sem.at[k], rr_sem.at[k], k, f).wait_recv()

    rv = rall[...].reshape(NJ * 16, LANES)
    lp = (iota((8, LANES), 1) >= HID) & (iota((8, LANES), 1) < HID + 3)
    like_row = dot_nt(jnp.where(lp, 1.0, 0.0).astype(BF16), rv)[0:1]
    zrow[...] = like_row

    @pl.loop(1, NF)
    def _(i):
        g = (f + i) % NF
        remote(zrow, zall.at[f], ls_sem.at[g], lr_sem.at[f], j, g).start()

    zall[f] = zrow[...]
    sall[f] = srow[...]

    @pl.loop(1, NF)
    def _(i):
        g = (f + i) % NF
        remote(srow, sall.at[g], ss_sem.at[g], sr_sem.at[g], j, g).wait_recv()
        remote(zrow, zall.at[g], ls_sem.at[g], lr_sem.at[g], j, g).wait_recv()

    total, score = zall[0], sall[0]
    for g in range(1, NF):
        total, score = total + zall[g], score + sall[g]
    mine = mine_s[...] > 0.5
    retrieve = jnp.broadcast_to(score, (64, 512)) * (1.0 / math.sqrt(2048.0))
    joined = retrieve + jnp.broadcast_to(total, (64, 512))

    def softmax(v):
        top = jnp.max(jnp.where(mine, v, -3.0e38), axis=1, keepdims=True)
        ex = jnp.where(mine, jnp.exp(jnp.where(mine, v - top, 0.0)), 0.0)
        norm = jnp.sum(ex, axis=1, keepdims=True)
        return ex / norm, top + jnp.log(norm)

    prior, lse_r = softmax(retrieve)
    post, lse_j = softmax(joined)
    loss = lse_r - lse_j
    own_row = (iota((64, 128), 0) == f * 8 + iota((64, 128), 1)) & (iota((64, 128), 1) < 4)
    loss_ref[...] = jnp.sum(jnp.where(own_row, loss, 0.0), axis=0, keepdims=True)[:, 0:4]

    hi, lo = two(post)
    mix = dot(hi, rv) + dot(lo, rv)
    mix = jnp.where(iota((64, LANES), 1) < HID, mix, 0.0)
    hi, lo = two(mix)
    fhi, flo = two((prior - post) * (LOSS_SCALE / math.sqrt(2048.0)))
    first = dot(fhi, ev_s[...]) + dot(flo, ev_s[...])
    upper = (iota((64, 256), 0) // 4) % 2 == 1
    for b in range(4):
        w_lo, w_hi = w2[b * 256 : (b + 1) * 256, :], w2[1024 + b * 256 : 1024 + (b + 1) * 256, :]
        part = jnp.where(upper, dot_nt(hi, w_hi) + dot_nt(lo, w_hi), dot_nt(hi, w_lo) + dot_nt(lo, w_lo))
        place = ((f % 4) == b) & (upper == (f // 4 == 1))
        part = jnp.where(place, first, 0.0) - LOSS_SCALE * part
        outp[b] = part.reshape(NF, 8, 256)

        @pl.loop(1, NF)
        def _(i):
            g = (f + i) % NF
            remote(outp.at[b, g], orec.at[b, f], os_sem.at[b, g], or_sem.at[b, f], j, g).start()

    for n, (slot, to) in enumerate(sent_w):
        block_copy(wall, gs_sem, gr_sem, slot, n, to).wait_send()

    for n, (slot, to) in enumerate(sent_q):
        block_copy(qw, hs_sem, hr_sem, slot, n, to).wait_send()

    @pl.loop(4, 16)
    def _(n):
        block_copy(qw, hs_sem, hr_sem, j, 24 + n, mate).wait_send()

    @pl.loop(0, 32)
    def _(n):
        @pl.when(n != 16)
        def _():
            block_copy(emball, es_sem, er_sem, j, n, mate).wait_send()

    @pl.loop(1, NJ)
    def _(i):
        k = (j + i) % NJ
        remote(rsend.at[k], rall.at[k], rs_sem.at[k], rr_sem.at[k], k, f).wait_send()

    @pl.loop(1, NF)
    def _(i):
        g = (f + i) % NF
        remote(wsl.at[g], wall.at[j, g], ws_sem.at[g], wr_sem.at[g], j, g).wait_send()
        remote(q_ref, qz.at[g], qs_sem.at[g], qr_sem.at[g], j, g).wait_send()
        remote(zrow, zall.at[g], ls_sem.at[g], lr_sem.at[g], j, g).wait_send()
        remote(srow, sall.at[g], ss_sem.at[g], sr_sem.at[g], j, g).wait_send()

    for b in range(4):

        @pl.loop(1, NF)
        def _(i):
            g = (f + i) % NF
            remote(outp.at[b, g], orec.at[b, g], os_sem.at[b, g], or_sem.at[b, g], j, g).wait()

        orec[b, f] = outp[b, f]
        whole = orec[b, 0]
        for g in range(1, NF):
            whole = whole + orec[b, g]
        grad_ref[:, b * 256 : (b + 1) * 256] = whole[0:4]
        grad_ref[:, 1024 + b * 256 : 1024 + (b + 1) * 256] = whole[4:8]


def on_device(queries, candidates, tables, lengths, passage_embed, reader_weight, readout):
    vm = pl.BlockSpec(memory_space=pltpu.VMEM)
    dma = pltpu.SemaphoreType.DMA
    grad, loss = pl.pallas_call(
        kernel,
        out_shape=(jax.ShapeDtypeStruct((4, 2048), F32), jax.ShapeDtypeStruct((1, 4), F32)),
        in_specs=[pl.BlockSpec(memory_space=pltpu.HBM)] * 7,
        out_specs=(vm, vm),
        scratch_shapes=[
            pltpu.VMEM((8, 2560), BF16),
            pltpu.VMEM((4, 2048), BF16),
            pltpu.VMEM((4, 8), I32),
            pltpu.VMEM((1, 32), I32),
            pltpu.VMEM((20, 128), F32),
            pltpu.VMEM((NF, 8, LANES), BF16),
            pltpu.VMEM((NF, 8, LANES), F32),
            pltpu.VMEM((NF, 4, 2048), BF16),
            pltpu.VMEM((NJ, NF, 8, LANES), BF16),
            pltpu.VMEM((2048, LANES), BF16),
            pltpu.VMEM((640, 2048), BF16),
            pltpu.VMEM((3, 832, 128), F32),
            pltpu.VMEM((32, 24, 256), F32),
            pltpu.VMEM((32, 16, 128), F32),
            pltpu.VMEM((NJ, 80, 128), F32),
            pltpu.VMEM((32, 128), F32),
            pltpu.VMEM((8, 512), I32),
            pltpu.SMEM((8, 512), I32),
            pltpu.VMEM((32, 128), F32),
            pltpu.VMEM((NJ, 32, 256), BF16),
            pltpu.VMEM((512, 256), BF16),
            pltpu.VMEM((64, 512), F32),
            pltpu.VMEM((2, 4, 128, 128), F32),
            pltpu.VMEM((2, 16, 128), F32),
            pltpu.VMEM((NJ, 16, LANES), BF16),
            pltpu.VMEM((NJ, 16, LANES), BF16),
            pltpu.VMEM((1, 512), F32),
            pltpu.VMEM((NF, 1, 512), F32),
            pltpu.VMEM((1, 512), F32),
            pltpu.VMEM((NF, 1, 512), F32),
            pltpu.VMEM((4, NF, 8, 256), F32),
            pltpu.VMEM((4, NF, 8, 256), F32),
            pltpu.VMEM((512, 128), F32),
            pltpu.VMEM((32, LANES), F32),
            dma((NF,)), dma((NF,)), dma((NF,)), dma((NF,)),
            dma((48,)), dma((NJ,)), dma((40,)), dma((NJ,)),
            dma((NJ,)), dma((NJ,)), dma((NJ,)), dma((NJ,)),
            dma((NF,)), dma((NF,)), dma((4, NF)), dma((4, NF)), dma((5,)), dma((7,)), dma((NF,)), dma((NF,)),
        ],
        compiler_params=pltpu.CompilerParams(collective_id=0, has_side_effects=True, vmem_limit_bytes=67043328),
    )(
        reader_weight,
        queries,
        candidates,
        tables.transpose(1, 0, 2).reshape(640, 2048),
        lengths.reshape(1, 32),
        passage_embed,
        readout.reshape(20, 128),
    )
    return grad, loss.reshape(4)


def solution(mesh):
    both = ("corpus", "fsdp")
    in_specs = (P(both, None), P(both, None), P("corpus", None, None), P("corpus"), P("corpus", None), P(both, None), P())
    return jax.shard_map(
        on_device, mesh=mesh, in_specs=in_specs, out_specs=(P(both, None), P(both)), check_vma=False
    )
```

time: 91.5 us -> 71.4 us (0.78); the launches traced: 90.3 us -> 71.3 us
  Pallas kernels: 82.3 us -> 68.1 us
  local copies, waits for them, and re-layouts: 7.3 us -> 2.55 us
    pallas_call x1, Pallas kernels: 82.3 us -> 68.1 us  [on_device(): pl.pallas_call(kernel, out_shape=(jax.ShapeDtypeStruct((4, 2048), F32), j...]
    unnamed x16 -> x2, local copies, waits for them, and re-layouts: 7.3 us -> 2.55 us
where the time goes in v2:
time: 71.4 us; the launch traced here: 71.3 us
  Pallas kernels  68.1 us (95%)
  local copies, waits for them, and re-layouts  2.55 us (4%)
    pallas_call x1, Pallas kernels, on_device(): pl.pallas_call(kernel, out_shape=(jax.ShapeDtypeStruct((4, 2048), F32), j...  68.1 us
    unnamed x2, local copies, waits for them, and re-layouts  2.55 us

profile of v2, /device:TPU:2, one launch (start us, length us, event | category | flops | bytes accessed | tf_op | source)
XLA Modules:
  0.0 71.3 jit_solution(1551095031470170966)
XLA Ops:
  0.6 68.1 %shard_map.86 = (f32[4,2048]{1,0:T(4,128)}, f32[1,4]{1,0:T(1,128)}) custom-call(bf16[8,2560]{1,0:T(8,128)(2,1)} %w_hbm.1, bf16[4,2048]{1,0:T(4,128)(2,1)} %q_hbm.1, s32[4,8]{1,0:T(4,128)} %cand_hbm.1, bf16[640,2048]{1,0:T(8,128)(2,1)} %bitcast.6, s32[1,32]{1,0:T(1,128)} %bitcast.8, bf16[32,2048]{1,0:T(8,128)(2,1)} %emb_hbm.1, f32[20,128]{1,0:T(8,128)} %bitcast.7), custom_call_target="tpu_custom_call" | custom-call | tf_op jit(solution)/shard_map/pallas_call | solution.py:491
  68.7 1.4 %copy.11 = f32[4,2048]{1,0:T(4,128)} copy(f32[4,2048]{1,0:T(4,128)} %get-tuple-element.8) | data formatting | bytes 65536
  70.1 1.2 %copy.12 = f32[4]{0:T(128)} copy(f32[4]{0:T(128)} %bitcast.9) | data formatting | bytes 32

commit v3 on v2

--- a/solution.py
+++ b/solution.py
@@ -45,7 +45,7 @@
     w_hbm, q_hbm, cand_hbm, tab_hbm, len_hbm, emb_hbm, ro_hbm,
     grad_ref, loss_ref,
     w_ref, q_ref, cand_ref, len_ref, ro_ref, wsl, ros, qz, wall, w2, x_s, tw0, tw, tw3, qw, linv, cidv, cid, lens_s, emball, ev_s, mine_s, acc, lvs, rsend, rall,
-    zrow, zall, srow, sall, outp, orec, tab, qcur,
+    zrow, zall, srow, sall, outp, orec, tab, qcur, q32,
     ws_sem, wr_sem, qs_sem, qr_sem, gs_sem, gr_sem, hs_sem, hr_sem, es_sem, er_sem, rs_sem, rr_sem,
     ls_sem, lr_sem, os_sem, or_sem, c_sem, i_sem, ss_sem, sr_sem,
 ):
@@ -154,6 +154,14 @@
     def wait_w(slot):
         block_copy(wall, gs_sem, gr_sem, slot, 0, mate).wait_recv()
 
+    def unpack(k):
+        for h in range(4):
+            pair = jnp.concatenate([wall[k, 2 * h].astype(F32), wall[k, 2 * h + 1].astype(F32)], axis=0)
+            w2[pl.ds(pl.multiple_of(k * 64 + h * 16, 16), 16), :] = pair.astype(BF16)
+            for e in range(2):
+                tab[pl.ds(k * 8 + 2 * h + e, 1), :] = pair[8 * e : 8 * e + 1, 256:LANES]
+                tab[pl.ds(256 + k * 8 + 2 * h + e, 1), :] = pair[8 * e + 1 : 8 * e + 2, 256:LANES]
+
     for a in near[1:]:
         send_w(j, chip[a, 0])
     for b in near[1:]:
@@ -168,6 +176,10 @@
         for b in near[1:]:
             send_w(chip[a, 0], chip[0, b])
         send_w(chip[a, 0], mate)
+    unpack(j)
+    for a in near[1:]:
+        unpack(chip[a, 0])
+
     r64, s64 = iota((64, 512), 0), iota((64, 512), 1)
     spread = jnp.where(iota((128, 512), 0) == HID - 256 + iota((128, 512), 1) // 16 * 2 + iota((128, 512), 1) % 2, 1.0, 0.0).astype(BF16)
     ids = [wall[j, g, :, 256:LANES].astype(F32) for g in range(NF)]
@@ -194,30 +206,32 @@
         for b in near[1:]:
             wait_w(chip[a, b])
             send_w(chip[a, b], mate)
+            unpack(chip[a, b])
+
+    own_q.wait()
+
+    @pl.loop(1, NF)
+    def _(i):
+        g = (f + i) % NF
+        remote(q_ref, qz.at[g], qs_sem.at[g], qr_sem.at[g], j, g).wait_recv()
+
+    q4 = [qz[g].astype(F32) for g in range(NF)]
+    q32[...] = jnp.concatenate(q4, axis=0).astype(BF16)
+    q64 = jnp.concatenate([qz[g, :, pl.ds(pl.multiple_of(f * 256, 256), 256)].astype(F32) for g in range(NF) for _ in range(2)], axis=0)
+    sc = dot_nt(q64.astype(BF16), ev_s[...])
+    srow[...] = jnp.sum(jnp.where((mine_s[...] > 0.5) & ((r64 // 4) % 2 == 0), sc, 0.0), axis=0, keepdims=True)
+
+    @pl.loop(1, NF)
+    def _(i):
+        g = (f + i) % NF
+        remote(srow, sall.at[f], ss_sem.at[g], sr_sem.at[f], j, g).start()
 
     @pl.loop(0, 16)
     def _(n):
         wait_w(n * 2 + 1 - jc)
-
-    @pl.loop(0, NJ)
-    def _(k):
-        for h in range(4):
-            pair = jnp.concatenate([wall[k, 2 * h].astype(F32), wall[k, 2 * h + 1].astype(F32)], axis=0)
-            w2[pl.ds(pl.multiple_of(k * 64 + h * 16, 16), 16), :] = pair.astype(BF16)
-            for e in range(2):
-                tab[pl.ds(k * 8 + 2 * h + e, 1), :] = pair[8 * e : 8 * e + 1, 256:LANES]
-                tab[pl.ds(256 + k * 8 + 2 * h + e, 1), :] = pair[8 * e + 1 : 8 * e + 2, 256:LANES]
-
-    own_q.wait()
-
-    @pl.loop(1, NF)
-    def _(i):
-        g = (f + i) % NF
-        remote(q_ref, qz.at[g], qs_sem.at[g], qr_sem.at[g], j, g).wait_recv()
-
-    q4 = [qz[g].astype(F32) for g in range(NF)]
-    q32 = jnp.concatenate(q4, axis=0).astype(BF16)
-    q_own = dot(q32, w2[...]) * GELU_SCALE
+        unpack(n * 2 + 1 - jc)
+
+    q_own = dot(q32[...], w2[...]) * GELU_SCALE
     qw[j, 0:32, :] = q_own[:, 0:128]
     qw[j, 32:64, :] = q_own[:, 128:256]
     third = jnp.where(iota((16, 128), 1) < 64, q_own[0:16, 256:384], pltpu.roll(q_own[16:32, 256:384], 64, 1))
@@ -269,15 +283,6 @@
             send_q(chip[a, 0], chip[0, b])
         send_q(chip[a, 0], mate)
     to_smem.wait()
-
-    q64 = jnp.concatenate([qz[g, :, pl.ds(pl.multiple_of(f * 256, 256), 256)].astype(F32) for g in range(NF) for _ in range(2)], axis=0)
-    sc = dot_nt(q64.astype(BF16), ev_s[...])
-    srow[...] = jnp.sum(jnp.where((mine_s[...] > 0.5) & ((r64 // 4) % 2 == 0), sc, 0.0), axis=0, keepdims=True)
-
-    @pl.loop(1, NF)
-    def _(i):
-        g = (f + i) % NF
-        remote(srow, sall.at[f], ss_sem.at[g], sr_sem.at[f], j, g).start()
 
     lane16 = iota((16, LANES), 1)
     ro16 = ros[f]
@@ -316,36 +321,22 @@
         summed = jnp.where(lane16 == HID + 2, low, summed)
         rsend[k] = summed.astype(BF16)
 
-    def is_mate(i):
-        return ((i % 2 == 0) & (i > 0)) | (i == NJ - 1)
-
-    def block_at(i):
-        p = jnp.where(is_mate(i), jnp.where(i == NJ - 1, 15, i // 2 - 1), (i + 1) // 2)
-        t = p - 7
-        m = jnp.where(p < 4, p, jnp.where(p < 7, 0, 1 + t % 3))
-        n = jnp.where(p < 4, 0, jnp.where(p < 7, p - 3, 1 + t // 3))
-        a, b = m + (m // 2) * (1 - 2 * (m % 2)), n + (n // 2) * (1 - 2 * (n % 2))
-        c = jnp.where(is_mate(i), 1 - jc, jc)
-        return at(jx + jnp.where(c == 0, a, b), jy + jnp.where(c == 0, b, a), c)
-
-    def do_block(i, half):
-        k = block_at(i)
-
-        @pl.when(is_mate(i) | ((i + 1) // 2 > 3))
-        def _():
-            block_copy(qw, hs_sem, hr_sem, k, 0, mate).wait_recv()
-
-        @pl.when((i > 0) & jnp.logical_not(is_mate(i)) & ((i + 1) // 2 > 3))
-        def _():
-            block_copy(qw, hs_sem, hr_sem, k, 24 + (i + 1) // 2, mate).start()
-
+    def ranked(r, c):
+        t = jnp.maximum(r - 7, 0)
+        m = jnp.where(r < 4, r, jnp.where(r < 7, 0, 1 + lax.rem(t, 3)))
+        n = jnp.where(r < 4, 0, jnp.where(r < 7, r - 3, 1 + lax.div(t, 3)))
+        m, n = jnp.where(m == 2, 3, jnp.where(m == 3, 2, m)), jnp.where(n == 2, 3, jnp.where(n == 3, 2, n))
+        x, y = jnp.where(c == 0, m, n), jnp.where(c == 0, n, m)
+        return lax.rem(jx + x, 4) * 8 + lax.rem(jy + y, 4) * 2 + c
+
+    def do_block(k, last, half, started):
         qcur[:, 0:128] = qw[k, 0:32, :]
         qcur[:, 128:256] = qw[k, 32:64, :]
         third = qw[k, 64:80, :]
         swap = pltpu.roll(third, 64, 1)
         qcur[0:16, 256:384] = jnp.where(iota((16, 128), 1) < 64, third, swap)
         qcur[16:32, 256:384] = jnp.where(iota((16, 128), 1) < 64, swap, third)
-        finish(1 - half, block_at((i + NJ - 1) % NJ))
+        finish(1 - half, last)
         for s in range(16):
             d, e = s // 2, s % 2
             c = jnp.clip(cid[e, k * 8 + d], 0, 31)
@@ -363,19 +354,31 @@
             acc[half, 3, at8, :] = value[:, 0:128] + value[:, 128:256] + value3
             lvs[half, pl.ds(s, 1), :] = linv[pl.ds(c, 1), :]
 
-        @pl.when(i > 1)
+        @pl.when(started)
         def _():
-            send_block(block_at(i - 1))
-
-    @pl.loop(0, NJ // 2)
-    def _(n):
-        do_block(2 * n, 0)
-        do_block(2 * n + 1, 1)
-
-    finish((NJ - 1) % 2, block_at(NJ - 1))
+            send_block(last)
+
+    def two_blocks(r, carry):
+        mine_k, last = carry
+        later = ranked(jnp.minimum(r + 1, 15), jc)
+
+        @pl.when((r > 2) & (r < 15))
+        def _():
+            block_copy(qw, hs_sem, hr_sem, later, 0, mate).wait_recv()
+            block_copy(qw, hs_sem, hr_sem, later, 24 + r, mate).start()
+
+        do_block(mine_k, last, 0, r > 0)
+        other_k = ranked(r, 1 - jc)
+        block_copy(qw, hs_sem, hr_sem, other_k, 0, mate).wait_recv()
+        do_block(other_k, mine_k, 1, r > 0)
+        return later, other_k
+
+    final_k = ranked(15, 1 - jc)
+    lax.fori_loop(0, 16, two_blocks, (j, final_k))
+    finish(1, final_k)
     own_r_copy = pltpu.make_async_copy(rsend.at[j], rall.at[j], c_sem.at[4])
     own_r_copy.start()
-    send_block(block_at(NJ - 1))
+    send_block(final_k)
 
     own_r_copy.wait()
 
@@ -422,16 +425,17 @@
     own_row = (iota((64, 128), 0) == f * 8 + iota((64, 128), 1)) & (iota((64, 128), 1) < 4)
     loss_ref[...] = jnp.sum(jnp.where(own_row, loss, 0.0), axis=0, keepdims=True)[:, 0:4]
 
-    hi, lo = two(post)
-    mix = dot(hi, rv) + dot(lo, rv)
+    mix = dot(jnp.concatenate(two(post), axis=0), rv)
+    mix = mix[0:64] + mix[64:128]
     mix = jnp.where(iota((64, LANES), 1) < HID, mix, 0.0)
-    hi, lo = two(mix)
-    fhi, flo = two((prior - post) * (LOSS_SCALE / math.sqrt(2048.0)))
-    first = dot(fhi, ev_s[...]) + dot(flo, ev_s[...])
+    mix = jnp.concatenate(two(mix), axis=0)
+    first = dot(jnp.concatenate(two((prior - post) * (LOSS_SCALE / math.sqrt(2048.0))), axis=0), ev_s[...])
+    first = first[0:64] + first[64:128]
     upper = (iota((64, 256), 0) // 4) % 2 == 1
     for b in range(4):
         w_lo, w_hi = w2[b * 256 : (b + 1) * 256, :], w2[1024 + b * 256 : 1024 + (b + 1) * 256, :]
-        part = jnp.where(upper, dot_nt(hi, w_hi) + dot_nt(lo, w_hi), dot_nt(hi, w_lo) + dot_nt(lo, w_lo))
+        up, down = dot_nt(mix, w_hi), dot_nt(mix, w_lo)
+        part = jnp.where(upper, up[0:64] + up[64:128], down[0:64] + down[64:128])
         place = ((f % 4) == b) & (upper == (f // 4 == 1))
         part = jnp.where(place, first, 0.0) - LOSS_SCALE * part
         outp[b] = part.reshape(NF, 8, 256)
@@ -447,7 +451,7 @@
     for n, (slot, to) in enumerate(sent_q):
         block_copy(qw, hs_sem, hr_sem, slot, n, to).wait_send()
 
-    @pl.loop(4, 16)
+    @pl.loop(3, 15)
     def _(n):
         block_copy(qw, hs_sem, hr_sem, j, 24 + n, mate).wait_send()
 
@@ -528,20 +532,26 @@
             pltpu.VMEM((4, NF, 8, 256), F32),
             pltpu.VMEM((512, 128), F32),
             pltpu.VMEM((32, LANES), F32),
+            pltpu.VMEM((32, 2048), BF16),
             dma((NF,)), dma((NF,)), dma((NF,)), dma((NF,)),
             dma((48,)), dma((NJ,)), dma((40,)), dma((NJ,)),
             dma((NJ,)), dma((NJ,)), dma((NJ,)), dma((NJ,)),
             dma((NF,)), dma((NF,)), dma((4, NF)), dma((4, NF)), dma((5,)), dma((7,)), dma((NF,)), dma((NF,)),
         ],
-        compiler_params=pltpu.CompilerParams(collective_id=0, has_side_effects=True, vmem_limit_bytes=67043328),
+        compiler_params=pltpu.CompilerParams(collective_id=0, has_side_effects=True, vmem_limit_bytes=40 << 20),
     )(
-        reader_weight,
-        queries,
-        candidates,
-        tables.transpose(1, 0, 2).reshape(640, 2048),
-        lengths.reshape(1, 32),
-        passage_embed,
-        readout.reshape(20, 128),
+        *[
+            pltpu.with_memory_space_constraint(v, pltpu.HBM)
+            for v in (
+                reader_weight,
+                queries,
+                candidates,
+                tables.transpose(1, 0, 2).reshape(640, 2048),
+                lengths.reshape(1, 32),
+                passage_embed,
+                readout.reshape(20, 128),
+            )
+        ]
     )
     return grad, loss.reshape(4)
 

time: 71.4 us -> 66.8 us (0.936)
  Pallas kernels: 68.1 us -> 65 us
  local copies, waits for them, and re-layouts: 2.55 us -> 1.13 us
    pallas_call x1, Pallas kernels: 68.1 us -> 65 us  [on_device(): pl.pallas_call(kernel, out_shape=(jax.ShapeDtypeStruct((4, 2048), F32), j...]
    unnamed x2, local copies, waits for them, and re-layouts: 2.55 us -> 1.13 us
where the time goes in v3:
time: 66.8 us; the launch traced here: 66.7 us
  Pallas kernels  65 us (97%)
  local copies, waits for them, and re-layouts  1.13 us (2%)
    pallas_call x1, Pallas kernels, on_device(): pl.pallas_call(kernel, out_shape=(jax.ShapeDtypeStruct((4, 2048), F32), j...  65 us

profile of v3, /device:TPU:2, one launch (start us, length us, event | category | flops | bytes accessed | tf_op | source)
XLA Modules:
  0.0 66.7 jit_solution(13393966143464029925)
XLA Ops:
  0.6 65.0 %shard_map.86 = (f32[4,2048]{1,0:T(4,128)S(1)}, f32[1,4]{1,0:T(1,128)S(1)}) custom-call(bf16[8,2560]{1,0:T(8,128)(2,1)} %w_hbm.1, bf16[4,2048]{1,0:T(4,128)(2,1)} %q_hbm.1, s32[4,8]{1,0:T(4,128)} %cand_hbm.1, bf16[640,2048]{1,0:T(8,128)(2,1)} %bitcast.7, s32[1,32]{1,0:T(1,128)} %bitcast.9, bf16[32,2048]{1,0:T(8,128)(2,1)} %emb_hbm.1, f32[20,128]{1,0:T(8,128)} %bitcast.8), custom_call_target="tpu_custom_call" | custom-call | tf_op jit(solution)/shard_map/pallas_call | solution.py:495
  65.6 0.6 copy.11
  66.2 0.5 copy.12
